TPU v7x, 128 devices: a whole 4x4x4 slice. The times are simulated.
128 devices in a mesh: dp: 16 (over z, y), mp: 8 (over x, core).
Axes of the slice: x: 4, y: 4, z: 4, core: 2. Of those that a mesh axis runs over, the one named last changes fastest.
Arguments:
- cotangent: bfloat16 [32768, 4096], P('dp'), may hold values from -64 to 64, as said below
- activation: bfloat16 [32768, 8192], P('dp', 'mp'), may hold values from -64 to 64, as said below
Outputs:
- update: bfloat16 [4096, 8192], P('dp', 'mp')
Inputs may be any that keep to these rules, and one draw needn't show every extreme that they name: `cotangent`: real-valued entries. `activation`: real-valued entries.
All inputs are finite; a program needn't handle non-finite values.
Results may differ from a plain program's by a relative error of at most 0.0054.
Values may be sent and summed in bfloat16 or wider, within the bound.
A program may use at most 256 MiB of HBM per device.

v0:
```python
import math
import jax
import jax.numpy as jnp
from jax import lax
from jax.sharding import PartitionSpec as P

N = 8192
ROWS = 4096
LINEAR_COEF = 3.4445
CUBIC_COEF = -4.775
QUINTIC_COEF = 2.0315
NORM_EPSILON = 1e-07
NORM_SHARE = 0.25
CONTRACT_FIRST = (((0,), (0,)), ((), ()))
CONTRACT_LAST = (((1,), (1,)), ((), ()))


def local(cotangent, activation):
    section = cotangent
    gradient = lax.psum_scatter(
        lax.dot_general(section, activation, CONTRACT_FIRST, preferred_element_type=jnp.float32),
        "dp",
        scatter_dimension=0,
        tiled=True,
    )
    sum_squares = lax.psum(jnp.sum(gradient * gradient), ("dp", "mp"))
    factor = NORM_SHARE * math.sqrt(ROWS) / (jnp.sqrt(sum_squares) + NORM_EPSILON)
    normalized = (gradient * factor).astype(jnp.bfloat16)
    weight_column = lax.all_gather(normalized, "dp", axis=0, tiled=True)
    section = weight_column
    gram_tile = lax.psum_scatter(
        lax.dot_general(section, normalized, CONTRACT_LAST, preferred_element_type=jnp.float32),
        "mp",
        scatter_dimension=0,
        tiled=True,
    ).T.astype(jnp.bfloat16)
    row_panel = lax.all_gather(gram_tile, "mp", axis=1, tiled=True)
    section = row_panel
    square_tile = jnp.dot(
        section,
        lax.all_gather(gram_tile, "dp", axis=0, tiled=True),
        preferred_element_type=jnp.float32,
    )
    polynomial = (CUBIC_COEF * gram_tile.astype(jnp.float32) + QUINTIC_COEF * square_tile).astype(
        jnp.bfloat16
    )
    section = weight_column
    product_tile = jnp.dot(
        lax.all_gather(polynomial, "mp", axis=1, tiled=True),
        section,
        preferred_element_type=jnp.float32,
    )
    rescale = math.sqrt(N)
    return (rescale * (LINEAR_COEF * normalized.astype(jnp.float32) + product_tile)).astype(
        jnp.bfloat16
    )


def solution(mesh):
    return jax.shard_map(
        local,
        mesh=mesh,
        in_specs=(P("dp", None), P("dp", "mp")),
        out_specs=P("dp", "mp"),
        check_vma=False,
    )
```

profile of v0, /device:TPU:1, one launch (start us, length us, event | category | flops | bytes accessed | tf_op | source)
XLA Modules:
  0.0 457.3 jit_solution(6413023268243869418)
XLA Ops:
  6.5 0.0 reduce-scatter.3.cloned.1.call-start
  6.5 23.7 %fusion.4 = f32[4096,1024]{1,0:T(8,128)} fusion(bf16[2048,4096]{1,0:T(8,128)(2,1)} %param.2, bf16[2048,1024]{1,0:T(8,128)(2,1)} %param.3), kind=kOutput, calls=%fused_computation.9 | convolution fusion | flops 17179869184 | bytes 37748736 | tf_op jit(solution)/shard_map/dot_general | solution.py:21
  30.3 0.0 reduce-scatter.3.cloned.1.call-update
  30.3 0.0 all-gather.5.cloned.1.call-start
  30.3 113.7 %reduce-scatter.3.cloned.1.call-done = f32[256,1024]{1,0:T(8,128)} async-done(((f32[4096,1024]{1,0:T(8,128)}), f32[256,1024]{1,0:T(8,128)}) %reduce-scatter.3.cloned.1.call-update) | async-done | bytes 1048592 | tf_op jit(solution)/shard_map/reduce_scatter | solution.py:20
  144.0 2.1 multiply_reduce_fusion
  146.1 64.8 %psum.7 = f32[]{:T(128)} all-reduce(f32[]{:T(128)} %multiply_reduce_fusion), channel_id=1, replica_groups=mesh['dp'=16,'mp'=8] {'dp','mp'}, use_global_device_ids=true, to_apply=%region_2.0 | all-reduce | flops 1 | bytes 8 | tf_op jit(solution)/shard_map/psum | solution.py:26
  211.6 2.1 multiply_convert_fusion
  213.7 0.0 all-gather.5.cloned.1.call-update
  213.7 0.0 reduce-scatter.5.cloned.1.call-start
  213.8 68.2 %all-gather.5.cloned.1.call-done = bf16[4096,1024]{1,0:T(8,128)(2,1)} async-done(((bf16[256,1024]{1,0:T(8,128)(2,1)}), bf16[4096,1024]{1,0:T(8,128)(2,1)}) %all-gather.5.cloned.1.call-update) | async-done | bytes 8388624 | tf_op jit(solution)/shard_map/all_gather | solution.py:29
  282.0 7.8 %fusion.5 = f32[4096,256]{1,0:T(8,128)} fusion(bf16[4096,1024]{1,0:T(8,128)(2,1)} %all-gather.5.cloned.1.call-done, bf16[256,1024]{1,0:T(8,128)(2,1)} %multiply_convert_fusion), kind=kOutput, calls=%fused_computation.10 | convolution fusion | flops 2147483648 | bytes 13107200 | tf_op jit(solution)/shard_map/dot_general | solution.py:32
  289.8 0.0 reduce-scatter.5.cloned.1.call-update
  289.8 0.0 all-gather.7.cloned.1.call-start
  289.9 34.7 %reduce-scatter.5.cloned.1.call-done = f32[512,256]{1,0:T(8,128)} async-done(((f32[4096,256]{1,0:T(8,128)}), f32[512,256]{1,0:T(8,128)}) %reduce-scatter.5.cloned.1.call-update) | async-done | bytes 524304 | tf_op jit(solution)/shard_map/reduce_scatter | solution.py:31
  324.5 1.8 convert_bitcast_fusion
  326.3 0.0 all-gather.7.cloned.1.call-update
  326.3 0.0 all-gather.9.cloned.1.call-start
  326.4 0.5 all-gather.9.cloned.1.call-update
  326.9 0.0 copy-start
  326.9 0.0 all-gather.11.cloned.1.call-start
  327.0 26.9 %all-gather.7.cloned.1.call-done = bf16[256,4096]{0,1:T(8,128)(2,1)} async-done(((bf16[256,512]{0,1:T(8,128)(2,1)}), bf16[256,4096]{0,1:T(8,128)(2,1)}) %all-gather.7.cloned.1.call-update) | async-done | bytes 2097168 | tf_op jit(solution)/shard_map/all_gather | solution.py:37
  353.9 58.8 %all-gather.9.cloned.1.call-done = bf16[4096,512]{0,1:T(8,128)(2,1)} async-done(((bf16[256,512]{0,1:T(8,128)(2,1)}), bf16[4096,512]{0,1:T(8,128)(2,1)}) %all-gather.9.cloned.1.call-update) | async-done | bytes 4194320 | tf_op jit(solution)/shard_map/all_gather | solution.py:41
  412.6 4.8 %fusion.3 = bf16[256,512]{0,1:T(8,128)(2,1)} fusion(bf16[4096,512]{0,1:T(8,128)(2,1)} %all-gather.9.cloned.1.call-done, bf16[256,4096]{0,1:T(8,128)(2,1)} %all-gather.7.cloned.1.call-done, bf16[256,512]{0,1:T(8,128)(2,1)} %convert_bitcast_fusion), kind=kOutput, calls=%fused_computation.5 | convolution fusion | flops 1074397184 | bytes 6815744 | tf_op jit(solution)/shard_map/dot_general | solution.py:39
  417.4 0.0 all-gather.11.cloned.1.call-update
  417.5 25.8 %all-gather.11.cloned.1.call-done = bf16[256,4096]{0,1:T(8,128)(2,1)} async-done(((bf16[256,512]{0,1:T(8,128)(2,1)}), bf16[256,4096]{0,1:T(8,128)(2,1)}) %all-gather.11.cloned.1.call-update) | async-done | bytes 2097168 | tf_op jit(solution)/shard_map/all_gather | solution.py:49
  443.3 0.0 copy-done
  443.3 7.2 %fusion.1 = bf16[256,1024]{1,0:T(8,128)(2,1)} fusion(bf16[256,4096]{0,1:T(8,128)(2,1)} %all-gather.11.cloned.1.call-done, bf16[4096,1024]{1,0:T(8,128)(2,1)} %all-gather.5.cloned.1.call-done, bf16[256,1024]{1,0:T(8,128)(2,1)S(1)} %copy-done), kind=kOutput, calls=%fused_computation.2 | convolution fusion | flops 2148794368 | bytes 11534336 | tf_op jit(solution)/shard_map/dot_general | solution.py:48
Async XLA Ops:
  6.5 137.5 %reduce-scatter.3.cloned.1.call-start = ((), (), s32[]{:S(2)}) async-start(), calls=%async_computation.2 | async-start | bytes 17825792 | tf_op jit(solution)/shard_map/reduce_scatter | solution.py:20
  30.3 251.7 %all-gather.5.cloned.1.call-start = ((), (), s32[]{:S(2)}) async-start(), calls=%async_computation.3 | async-start | bytes 8912896 | tf_op jit(solution)/shard_map/all_gather | solution.py:29
  213.7 110.8 %reduce-scatter.5.cloned.1.call-start = ((), (), s32[]{:S(2)}) async-start(), calls=%async_computation.4 | async-start | bytes 4718592 | tf_op jit(solution)/shard_map/reduce_scatter | solution.py:31
  289.8 64.1 %all-gather.7.cloned.1.call-start = ((), (), s32[]{:S(2)}) async-start(), calls=%async_computation.5 | async-start | bytes 2359296 | tf_op jit(solution)/shard_map/all_gather | solution.py:37
  326.3 86.3 %all-gather.9.cloned.1.call-start = ((), (), s32[]{:S(2)}) async-start(), calls=%async_computation.6 | async-start | bytes 4456448 | tf_op jit(solution)/shard_map/all_gather | solution.py:41
  326.9 116.3 %copy-start = (bf16[256,1024]{1,0:T(8,128)(2,1)S(1)}, bf16[256,1024]{1,0:T(8,128)(2,1)}, u32[]{:S(2)}) copy-start(bf16[256,1024]{1,0:T(8,128)(2,1)} %multiply_convert_fusion) | copy-start | bytes 1572868
  326.9 116.3 %all-gather.11.cloned.1.call-start = ((), (), s32[]{:S(2)}) async-start(), calls=%async_computation.7 | async-start | bytes 2359296 | tf_op jit(solution)/shard_map/all_gather | solution.py:49
Sparse Core Ops, SparseCore 0:
  30.4 113.5 reduce-scatter.2
  213.9 68.1 all-gather.4
  289.9 34.5 reduce-scatter.4
  326.5 27.3 all-gather.6
  355.8 56.7 all-gather.8
  417.6 25.6 all-gather.10
where the time goes:
time: 458 us; the launch traced here: 457 us
  waiting for transfers between devices  329 us (72%)
  blocking collectives  64.8 us (14%)
  matrix products  43.5 us (9%)
  between operations  14.2 us (3%)
  other arithmetic  6 us (1%)
    reduce_scatter x1, waiting for transfers between devices, local(): lax.psum_scatter(lax.dot_general(section, activation, CONTRACT_FIRST, pre...  114 us
    all_gather x1, waiting for transfers between devices, local(): weight_column = lax.all_gather(normalized, 'dp', axis=0, tiled=True)  68.2 us
    psum x1, blocking collectives, local(): sum_squares = lax.psum(jnp.sum(gradient * gradient), ('dp', 'mp'))  64.8 us
    all_gather x1, waiting for transfers between devices, local(): lax.all_gather(gram_tile, 'dp', axis=0, tiled=True)  58.8 us
    reduce_scatter x1, waiting for transfers between devices, local(): lax.psum_scatter(lax.dot_general(section, normalized, CONTRACT_LAST, pref...  34.7 us
    all_gather x1, waiting for transfers between devices, local(): row_panel = lax.all_gather(gram_tile, 'mp', axis=1, tiled=True)  26.9 us
    all_gather x1, waiting for transfers between devices, local(): lax.all_gather(polynomial, 'mp', axis=1, tiled=True)  25.8 us
    dot_general x1, matrix products, local(): lax.dot_general(section, activation, CONTRACT_FIRST, preferred_element_ty...  23.7 us
  transfers between devices with their start and end apart: 6, of which 6 were waited for; matrix products, arithmetic and copies ran while one was open for 0% of the time, Pallas kernels for 0%

commit v1 on v0

--- a/solution.py
+++ b/solution.py
@@ -13,6 +13,11 @@
 NORM_SHARE = 0.25
 CONTRACT_FIRST = (((0,), (0,)), ((), ()))
 CONTRACT_LAST = (((1,), (1,)), ((), ()))
+
+
+def gather_over(x, name, d):
+    outgoing = jnp.stack([x] * lax.axis_size(name))
+    return jnp.concatenate(lax.all_to_all(outgoing, name, 0, 0), axis=d)
 
 
 def local(cotangent, activation):
@@ -34,7 +39,7 @@
         scatter_dimension=0,
         tiled=True,
     ).T.astype(jnp.bfloat16)
-    row_panel = lax.all_gather(gram_tile, "mp", axis=1, tiled=True)
+    row_panel = gather_over(gram_tile, "mp", 1)
     section = row_panel
     square_tile = jnp.dot(
         section,

time: 458 us -> 429 us (0.937)
  waiting for transfers between devices: 329 us -> 268 us
  blocking collectives: 64.8 us -> 97.3 us
    all_gather x1, waiting for transfers between devices: 58.8 us -> 25.2 us  [local(): lax.all_gather(gram_tile, 'dp', axis=0, tiled=True)]
    all_to_all x0 -> x1, blocking collectives: none -> 32.5 us  [gather_over(): return jnp.concatenate(lax.all_to_all(outgoing, name, 0, 0), axis=d)]
    all_gather x1 -> x0, waiting for transfers between devices: 26.9 us -> none  [local(): row_panel = lax.all_gather(gram_tile, 'mp', axis=1, tiled=True)]
  transfers between devices with their start and end apart: 6 -> 5, of which waited for: 6 -> 5; matrix products, arithmetic and copies ran while one was open for 0% -> 0% of each run, Pallas kernels for 0% -> 0%
where the time goes in v1:
time: 429 us
  waiting for transfers between devices  268 us (62%)
  blocking collectives  97.3 us (23%)
  matrix products  42.9 us (10%)
  between operations  13.9 us (3%)
  other arithmetic  6 us (1%)
    reduce_scatter x1, waiting for transfers between devices, local(): lax.psum_scatter(lax.dot_general(section, activation, CONTRACT_FIRST, pre...  114 us
    all_gather x1, waiting for transfers between devices, local(): weight_column = lax.all_gather(normalized, 'dp', axis=0, tiled=True)  68.2 us
    psum x1, blocking collectives, local(): sum_squares = lax.psum(jnp.sum(gradient * gradient), ('dp', 'mp'))  64.7 us
    reduce_scatter x1, waiting for transfers between devices, local(): lax.psum_scatter(lax.dot_general(section, normalized, CONTRACT_LAST, pref...  34.7 us
    all_to_all x1, blocking collectives, gather_over(): return jnp.concatenate(lax.all_to_all(outgoing, name, 0, 0), axis=d)  32.5 us
    all_gather x1, waiting for transfers between devices, local(): lax.all_gather(polynomial, 'mp', axis=1, tiled=True)  25.8 us
    all_gather x1, waiting for transfers between devices, local(): lax.all_gather(gram_tile, 'dp', axis=0, tiled=True)  25.2 us
    dot_general x1, matrix products, local(): lax.dot_general(section, activation, CONTRACT_FIRST, preferred_element_ty...  23.7 us
  transfers between devices with their start and end apart: 5, of which 5 were waited for; matrix products, arithmetic and copies ran while one was open for 0% of the time, Pallas kernels for 0%

profile of v1, /device:TPU:1, one launch (start us, length us, event | category | flops | bytes accessed | tf_op | source)
XLA Modules:
  0.0 428.9 jit_solution(605442620685837979)
XLA Ops:
  6.5 0.0 reduce-scatter.3.cloned.1.call-start
  6.5 23.7 %fusion.4 = f32[4096,1024]{1,0:T(8,128)} fusion(bf16[2048,4096]{1,0:T(8,128)(2,1)} %param.2, bf16[2048,1024]{1,0:T(8,128)(2,1)} %param.3), kind=kOutput, calls=%fused_computation.9 | convolution fusion | flops 17179869184 | bytes 37748736 | tf_op jit(solution)/shard_map/dot_general | solution.py:26
  30.3 0.0 reduce-scatter.3.cloned.1.call-update
  30.3 0.0 all-gather.4.cloned.1.call-start
  30.4 113.7 %reduce-scatter.3.cloned.1.call-done = f32[256,1024]{1,0:T(8,128)} async-done(((f32[4096,1024]{1,0:T(8,128)}), f32[256,1024]{1,0:T(8,128)}) %reduce-scatter.3.cloned.1.call-update) | async-done | bytes 1048592 | tf_op jit(solution)/shard_map/reduce_scatter | solution.py:25
  144.0 2.1 multiply_reduce_fusion
  146.1 64.7 %psum.7 = f32[]{:T(128)} all-reduce(f32[]{:T(128)} %multiply_reduce_fusion), channel_id=1, replica_groups=mesh['dp'=16,'mp'=8] {'dp','mp'}, use_global_device_ids=true, to_apply=%region_2.0 | all-reduce | flops 1 | bytes 8 | tf_op jit(solution)/shard_map/psum | solution.py:31
  211.6 2.1 multiply_convert_fusion
  213.7 0.0 all-gather.4.cloned.1.call-update
  213.7 0.0 reduce-scatter.5.cloned.1.call-start
  213.8 68.2 %all-gather.4.cloned.1.call-done = bf16[4096,1024]{1,0:T(8,128)(2,1)} async-done(((bf16[256,1024]{1,0:T(8,128)(2,1)}), bf16[4096,1024]{1,0:T(8,128)(2,1)}) %all-gather.4.cloned.1.call-update) | async-done | bytes 8388624 | tf_op jit(solution)/shard_map/all_gather | solution.py:34
  282.0 7.8 %fusion.5 = f32[4096,256]{1,0:T(8,128)} fusion(bf16[4096,1024]{1,0:T(8,128)(2,1)} %all-gather.4.cloned.1.call-done, bf16[256,1024]{1,0:T(8,128)(2,1)} %multiply_convert_fusion), kind=kOutput, calls=%fused_computation.10 | convolution fusion | flops 2147483648 | bytes 13107200 | tf_op jit(solution)/shard_map/dot_general | solution.py:37
  289.8 0.0 reduce-scatter.5.cloned.1.call-update
  289.8 0.0 all-gather.6.cloned.1.call-start
  289.9 34.7 %reduce-scatter.5.cloned.1.call-done = f32[512,256]{1,0:T(8,128)} async-done(((f32[4096,256]{1,0:T(8,128)}), f32[512,256]{1,0:T(8,128)}) %reduce-scatter.5.cloned.1.call-update) | async-done | bytes 524304 | tf_op jit(solution)/shard_map/reduce_scatter | solution.py:36
  324.5 1.8 convert_bitcast_fusion
  326.3 0.0 copy-start.1
  326.3 0.0 all-gather.6.cloned.1.call-update
  326.3 0.0 all-gather.8.cloned.1.call-start
  326.4 1.1 stack.2
  327.5 32.5 %all_to_all.5 = bf16[8,256,512]{1,2,0:T(8,128)(2,1)S(1)} all-to-all(bf16[8,256,512]{1,2,0:T(8,128)(2,1)S(1)} %stack.2), channel_id=1, replica_groups=mesh['dp'=16,'mp'=8] {'mp'}, dimensions={0} | all-to-all | bytes 4194304 | tf_op jit(solution)/shard_map/all_to_all | solution.py:20
  360.0 25.2 %all-gather.6.cloned.1.call-done = bf16[4096,512]{0,1:T(8,128)(2,1)} async-done(((bf16[256,512]{0,1:T(8,128)(2,1)}), bf16[4096,512]{0,1:T(8,128)(2,1)}) %all-gather.6.cloned.1.call-update) | async-done | bytes 4194320 | tf_op jit(solution)/shard_map/all_gather | solution.py:46
  385.2 0.0 copy-done.1
  385.2 0.0 copy-start
  385.2 4.2 fusion.3
  389.4 0.0 all-gather.8.cloned.1.call-update
  389.4 25.8 %all-gather.8.cloned.1.call-done = bf16[256,4096]{0,1:T(8,128)(2,1)} async-done(((bf16[256,512]{0,1:T(8,128)(2,1)}), bf16[256,4096]{0,1:T(8,128)(2,1)}) %all-gather.8.cloned.1.call-update) | async-done | bytes 2097168 | tf_op jit(solution)/shard_map/all_gather | solution.py:54
  415.2 0.0 copy-done
  415.2 7.2 %fusion.1 = bf16[256,1024]{1,0:T(8,128)(2,1)} fusion(bf16[256,4096]{0,1:T(8,128)(2,1)} %all-gather.8.cloned.1.call-done, bf16[4096,1024]{1,0:T(8,128)(2,1)} %all-gather.4.cloned.1.call-done, bf16[256,1024]{1,0:T(8,128)(2,1)S(1)} %copy-done), kind=kOutput, calls=%fused_computation.2 | convolution fusion | flops 2148794368 | bytes 11534336 | tf_op jit(solution)/shard_map/dot_general | solution.py:53
Async XLA Ops:
  6.5 137.5 %reduce-scatter.3.cloned.1.call-start = ((), (), s32[]{:S(2)}) async-start(), calls=%async_computation.3 | async-start | bytes 17825792 | tf_op jit(solution)/shard_map/reduce_scatter | solution.py:25
  30.3 251.7 %all-gather.4.cloned.1.call-start = ((), (), s32[]{:S(2)}) async-start(), calls=%async_computation.4 | async-start | bytes 8912896 | tf_op jit(solution)/shard_map/all_gather | solution.py:34
  213.7 110.8 %reduce-scatter.5.cloned.1.call-start = ((), (), s32[]{:S(2)}) async-start(), calls=%async_computation.5 | async-start | bytes 4718592 | tf_op jit(solution)/shard_map/reduce_scatter | solution.py:36
  289.8 95.4 %all-gather.6.cloned.1.call-start = ((), (), s32[]{:S(2)}) async-start(), calls=%async_computation.6 | async-start | bytes 4456448 | tf_op jit(solution)/shard_map/all_gather | solution.py:46
  326.3 58.9 %copy-start.1 = (bf16[256,512]{0,1:T(8,128)(2,1)S(1)}, bf16[256,512]{0,1:T(8,128)(2,1)}, u32[]{:S(2)}) copy-start(bf16[256,512]{0,1:T(8,128)(2,1)} %convert_bitcast_fusion) | copy-start | bytes 786436
  326.3 88.9 %all-gather.8.cloned.1.call-start = ((), (), s32[]{:S(2)}) async-start(), calls=%async_computation.7 | async-start | bytes 2359296 | tf_op jit(solution)/shard_map/all_gather | solution.py:54
  385.2 30.0 %copy-start = (bf16[256,1024]{1,0:T(8,128)(2,1)S(1)}, bf16[256,1024]{1,0:T(8,128)(2,1)}, u32[]{:S(2)}) copy-start(bf16[256,1024]{1,0:T(8,128)(2,1)} %multiply_convert_fusion) | copy-start | bytes 1572868
Sparse Core Ops, SparseCore 0:
  30.4 113.5 reduce-scatter.2
  213.9 68.1 all-gather.3
  289.9 34.5 reduce-scatter.4
  326.5 58.6 all-gather.5
  389.5 25.6 all-gather.7
